TPU v7x, 512 devices: a whole 4x4x16 slice. The times are simulated.
512 devices in a mesh: ctx: 64 (over y, x, z_lo), tp: 8 (over z_hi, core).
Axes of the slice: x: 4, y: 4, z: 16 (z_hi: 4, z_lo: 4; z = z_hi * 4 + z_lo), core: 2. Of those that a mesh axis runs over, the one named last changes fastest.
Arguments:
- tokens: bfloat16 [1920, 32768], P('tp', 'ctx'), may hold values from -6 to 6
- norm_gain: float32 [1920], replicated, may hold values from 0.1 to 1.9
- w_in: bfloat16 [3, 1920, 1920], P(None, 'tp'), may hold values from -0.125 to 0.125
- w_short: float32 [3, 3, 1920], P(None, None, 'tp'), may hold values from -3 to 3
- decay_rate: float32 [16, 1920], P(None, 'tp'), as said below
- residue: float32 [16, 1920], P(None, 'tp'), may hold values from -1.5 to 1.5
- skip_gain: float32 [1920], P('tp'), may hold values from -3 to 3
- w_out: bfloat16 [1920, 1920], P('tp'), may hold values from -0.125 to 0.125
Outputs:
- mixed: bfloat16 [1920, 32768], P('tp', 'ctx')
Inputs may be any that keep to these rules, and one draw needn't show every extreme that they name: `decay_rate`: every rate lies between 0.2 / 32768 and 1 / 30.
All inputs are finite; a program needn't handle non-finite values.
Results may differ from a plain program's by a relative error of at most 0.0077.
Values may be sent and summed in bfloat16 or wider, within the bound.
A program may use at most 64 MiB of HBM per device.

v0:
```python
import math

import jax
import jax.numpy as jnp
from jax import lax
from jax.sharding import PartitionSpec as P

highest = lax.Precision.HIGHEST


def shifted(value, axis, steps):
    count = lax.axis_size(axis)
    first, last = (max(0, -steps), min(count, count - steps))
    return lax.ppermute(value, axis, [(source, source + steps) for source in range(first, last)])


def angle_table(left, right, period):
    phase = left[:, None] * right[None, :] % period
    theta = phase.astype(jnp.float32) * (2.0 * math.pi / period)
    return (jnp.cos(theta), jnp.sin(theta))


def forward_spectrum(fields, part_count, position):
    count, row_count, local_width = fields.shape
    share_rows = row_count // part_count
    padded = 2 * part_count
    length_all = padded * row_count
    blocks = lax.all_to_all(
        fields.reshape(count, 1, row_count, local_width),
        "ctx",
        split_axis=2,
        concat_axis=1,
        tiled=True,
    )
    outer_cos, outer_sin = angle_table(
        jnp.arange(padded, dtype=jnp.int32), jnp.arange(part_count, dtype=jnp.int32), padded
    )
    real_first = jnp.einsum("kp,fpmc->fkmc", outer_cos, blocks, precision=highest)
    imag_first = -jnp.einsum("kp,fpmc->fkmc", outer_sin, blocks, precision=highest)
    offsets = position * share_rows + jnp.arange(share_rows, dtype=jnp.int32)
    twist_cos, twist_sin = angle_table(jnp.arange(padded, dtype=jnp.int32), offsets, length_all)
    twist_cos = twist_cos[None, :, :, None]
    twist_sin = twist_sin[None, :, :, None]
    real_second = real_first * twist_cos + imag_first * twist_sin
    imag_second = imag_first * twist_cos - real_first * twist_sin
    arrived = lax.all_to_all(
        jnp.stack([real_second, imag_second], 1), "ctx", split_axis=2, concat_axis=3, tiled=True
    )
    inner_cos, inner_sin = angle_table(
        jnp.arange(row_count, dtype=jnp.int32), jnp.arange(row_count, dtype=jnp.int32), row_count
    )
    real_in = arrived[:, 0]
    imag_in = arrived[:, 1]
    real_out = jnp.einsum("km,fjmc->fjkc", inner_cos, real_in, precision=highest) + jnp.einsum(
        "km,fjmc->fjkc", inner_sin, imag_in, precision=highest
    )
    imag_out = jnp.einsum("km,fjmc->fjkc", inner_cos, imag_in, precision=highest) - jnp.einsum(
        "km,fjmc->fjkc", inner_sin, real_in, precision=highest
    )
    return (real_out, imag_out)


def inverse_spectrum(real_part, imag_part, part_count, position):
    pair_count, row_count, local_width = real_part.shape
    padded = 2 * part_count
    length_all = padded * row_count
    inner_cos, inner_sin = angle_table(
        jnp.arange(row_count, dtype=jnp.int32), jnp.arange(row_count, dtype=jnp.int32), row_count
    )
    real_first = jnp.einsum("mk,jkc->jmc", inner_cos, real_part, precision=highest) - jnp.einsum(
        "mk,jkc->jmc", inner_sin, imag_part, precision=highest
    )
    imag_first = jnp.einsum("mk,jkc->jmc", inner_sin, real_part, precision=highest) + jnp.einsum(
        "mk,jkc->jmc", inner_cos, imag_part, precision=highest
    )
    lows = 2 * position + jnp.arange(2, dtype=jnp.int32)
    twist_cos, twist_sin = angle_table(lows, jnp.arange(row_count, dtype=jnp.int32), length_all)
    twist_cos = twist_cos[:, :, None]
    twist_sin = twist_sin[:, :, None]
    real_second = real_first * twist_cos - imag_first * twist_sin
    imag_second = real_first * twist_sin + imag_first * twist_cos
    arrived = lax.all_to_all(
        jnp.stack([real_second, imag_second], 0), "ctx", split_axis=2, concat_axis=1, tiled=True
    )
    outer_cos, outer_sin = angle_table(
        jnp.arange(part_count, dtype=jnp.int32), jnp.arange(padded, dtype=jnp.int32), padded
    )
    values = (
        jnp.einsum("pk,kmc->pmc", outer_cos, arrived[0], precision=highest)
        - jnp.einsum("pk,kmc->pmc", outer_sin, arrived[1], precision=highest)
    ) / length_all
    returned = lax.all_to_all(values, "ctx", split_axis=0, concat_axis=1, tiled=True)
    return returned.reshape(row_count, local_width)


def body(tokens, norm_gain, w_in, w_short, decay_rate, residue, skip_gain, w_out):
    row_count = tokens.shape[1]
    tap_count = w_short.shape[0]
    local_channels = w_in.shape[1]
    part_count = lax.axis_size("ctx")
    position = lax.axis_index("ctx")
    features = lax.all_gather(tokens, "tp", axis=0, tiled=True).astype(jnp.float32)
    row_scale = lax.rsqrt(jnp.mean(features * features, axis=0, keepdims=True) + 1e-06)
    normed = (features * row_scale * norm_gain[:, None]).astype(jnp.bfloat16)
    in_matrix = w_in.reshape(3 * local_channels, w_in.shape[2])
    projected = (
        jnp.dot(in_matrix, normed, preferred_element_type=jnp.float32)
        .astype(jnp.bfloat16)
        .reshape(3, local_channels, row_count)
    )
    earlier = shifted(projected[:, :, row_count - (tap_count - 1) :], "ctx", 1)
    extended = jnp.concatenate([earlier, projected], axis=2).astype(jnp.float32)
    short_mix = w_short[0][:, :, None] * extended[:, :, tap_count - 1 :]
    for offset in range(1, tap_count):
        start_row = tap_count - 1 - offset
        short_mix = (
            short_mix
            + w_short[offset][:, :, None] * extended[:, :, start_row : start_row + row_count]
        )
    query_stream = short_mix[0].T
    signal = (short_mix[1] * short_mix[2]).T
    mode_gains = residue * jnp.sqrt(-jnp.expm1(-2.0 * decay_rate))
    positions = (position * row_count + jnp.arange(row_count, dtype=jnp.int32)).astype(jnp.float32)
    filter_time = jnp.sum(
        mode_gains[None] * jnp.exp(-decay_rate[None] * positions[:, None, None]), axis=1
    )
    real_all, imag_all = forward_spectrum(jnp.stack([signal, filter_time], 0), part_count, position)
    real_signal, imag_signal = (real_all[0], imag_all[0])
    real_filter, imag_filter = (real_all[1], imag_all[1])
    real_product = real_signal * real_filter - imag_signal * imag_filter
    imag_product = real_signal * imag_filter + imag_signal * real_filter
    long_conv = inverse_spectrum(real_product, imag_product, part_count, position)
    gated = (query_stream * (long_conv + skip_gain * signal)).astype(jnp.bfloat16)
    partial_terms = lax.dot_general(
        w_out, gated, (((0,), (1,)), ((), ())), preferred_element_type=jnp.float32
    )
    summed = lax.psum_scatter(partial_terms, "tp", scatter_dimension=0, tiled=True)
    return summed.astype(jnp.bfloat16)


def solution(mesh):
    placed = (
        P("tp", "ctx"),
        P(),
        P(None, "tp", None),
        P(None, None, "tp"),
        P(None, "tp"),
        P(None, "tp"),
        P("tp"),
        P("tp", None),
    )
    return jax.shard_map(
        body, mesh=mesh, in_specs=placed, out_specs=P("tp", "ctx"), check_vma=False
    )
```

profile of v0, /device:TPU:25, one launch (start us, length us, event | category | flops | bytes accessed | tf_op | source)
XLA Modules:
  0.0 514.9 jit_solution(2655813005271735730)
XLA Ops:
  6.5 0.7 all-gather.2.cloned.1.call-update
  7.3 0.8 sqrt_multiply_fusion
  8.1 1.6 multiply_reduce_fusion
  9.7 65.5 %all-gather.2.cloned.1.call-done = bf16[1920,512]{1,0:T(8,128)(2,1)} async-done(((bf16[240,512]{1,0:T(8,128)(2,1)}), bf16[1920,512]{1,0:T(8,128)(2,1)}) %all-gather.2.cloned.1.call-update) | async-done | bytes 1966096 | tf_op jit(solution)/shard_map/all_gather | solution.py:102
  75.2 2.2 fusion
  77.4 1.8 fusion.17
  79.3 1.9 collective-permute-start
  81.2 10.7 %collective-permute-done = bf16[3,240,2]{2,1,0:T(8,128)(2,1)S(1)} collective-permute-done((bf16[3,240,2]{2,1,0:T(8,128)(2,1)S(1)}, bf16[3,240,2]{2,1,0:T(8,128)(2,1)S(1)}, u32[]{:S(2)}, u32[]{:S(2)}) %collective-permute-start) | collective-permute-done | bytes 2912 | tf_op jit(solution)/shard_map/ppermute | solution.py:14
  91.9 0.4 maximum_convert_fusion
  92.3 1.2 fusion.15
  93.6 1.1 copy-done.2
  94.9 1.3 copy.65
  96.2 5.5 %all-to-all-start = ((f32[2,1,512,240]{3,0,1,2:T(2,128)}), f32[2,1,512,240]{3,0,1,2:T(2,128)S(1)}, u32[]{:S(2)}, u32[]{:S(2)}) async-start(f32[2,1,512,240]{3,0,1,2:T(2,128)} %copy.65), calls=%async_computation | async-start | bytes 2097152 | tf_op jit(solution)/shard_map/all_to_all | solution.py:28
  101.8 26.2 %all-to-all-done = f32[2,1,512,240]{3,0,1,2:T(2,128)S(1)} async-done(((f32[2,1,512,240]{3,0,1,2:T(2,128)}), f32[2,1,512,240]{3,0,1,2:T(2,128)S(1)}, u32[]{:S(2)}, u32[]{:S(2)}) %all-to-all-start) | async-done | bytes 983072 | tf_op jit(solution)/shard_map/all_to_all | solution.py:28
  128.1 3.4 fusion.40
  131.5 3.5 fusion.10
  135.0 2.2 pad_maximum_fusion
  137.1 5.4 %copy.69 = f32[2,2,128,8,240]{4,3,0,1,2:T(8,128)} copy(f32[2,2,128,8,240]{2,4,3,0,1:T(8,128)} %pad_maximum_fusion) | data formatting | bytes 7864320 | tf_op jit(solution)/shard_map/stack | solution.py:47
  142.6 7.6 %all-to-all-start.1 = ((f32[2,2,128,8,240]{4,3,0,1,2:T(8,128)}), f32[2,2,128,8,240]{4,3,0,1,2:T(8,128)}, u32[]{:S(2)}, u32[]{:S(2)}) async-start(f32[2,2,128,8,240]{4,3,0,1,2:T(8,128)} %copy.69), calls=%async_computation.1 | async-start | bytes 8388608 | tf_op jit(solution)/shard_map/all_to_all | solution.py:46
  150.1 0.3 reduce-scatter.4.cloned.1.call-start
  150.4 0.2 fusion.98
  150.6 92.6 %all-to-all-done.1 = f32[2,2,128,8,240]{4,3,0,1,2:T(8,128)} async-done(((f32[2,2,128,8,240]{4,3,0,1,2:T(8,128)}), f32[2,2,128,8,240]{4,3,0,1,2:T(8,128)}, u32[]{:S(2)}, u32[]{:S(2)}) %all-to-all-start.1) | async-done | bytes 3932192 | tf_op jit(solution)/shard_map/all_to_all | solution.py:46
  243.1 2.6 copy.105
  245.7 10.4 %fusion.4 = f32[2,2,240,512]{3,2,1,0:T(8,128)S(1)} fusion(f32[2,2,2,512,240]{4,3,2,1,0:T(8,128)S(1)} %bitcast.166), kind=kOutput, calls=%fused_computation.13 | convolution fusion | flops 3023568896 | bytes 4063232 | tf_op jit(solution)/shard_map/km,fjmc->fjkc/dot_general | solution.py:54
  256.1 10.8 %fusion.3 = f32[2,2,240,512]{3,2,1,0:T(8,128)S(1)} fusion(f32[2,2,2,512,240]{4,3,2,1,0:T(8,128)S(1)} %bitcast.167), kind=kOutput, calls=%fused_computation.12 | convolution fusion | flops 3023568896 | bytes 4063232 | tf_op jit(solution)/shard_map/km,fjmc->fjkc/dot_general | solution.py:57
  267.0 10.6 %add_bitcast_fusion = f32[2,2,512,240]{2,3,1,0:T(8,128)S(1)} fusion(f32[2,2,240,512]{3,2,1,0:T(8,128)S(1)} %fusion.4, f32[2,2,2,512,240]{4,3,2,1,0:T(8,128)S(1)} %bitcast.168), kind=kOutput, calls=%fused_computation.27 | convolution fusion | flops 3024060416 | bytes 6029312 | tf_op jit(solution)/shard_map/km,fjmc->fjkc/dot_general | solution.py:54
  277.6 10.8 %subtract_bitcast_fusion = f32[2,2,512,240]{2,3,1,0:T(8,128)S(1)} fusion(f32[2,2,240,512]{3,2,1,0:T(8,128)S(1)} %fusion.3, f32[2,2,2,512,240]{4,3,2,1,0:T(8,128)S(1)} %bitcast.169), kind=kOutput, calls=%fused_computation.26 | convolution fusion | flops 3024060416 | bytes 6029312 | tf_op jit(solution)/shard_map/km,fjmc->fjkc/dot_general | solution.py:57
  288.5 0.5 multiply_add_fusion
  289.0 6.2 %fusion.24 = f32[2,240,512]{2,1,0:T(8,128)S(1)} fusion(f32[1,2,512,240]{2,3,1,0:T(8,128)S(1)} %get-tuple-element.8), kind=kOutput, calls=%fused_computation.46 | convolution fusion | flops 1513619456 | bytes 1966080 | tf_op jit(solution)/shard_map/mk,jkc->jmc/dot_general | solution.py:73
  295.2 6.2 %fusion.28 = f32[2,240,512]{2,1,0:T(8,128)S(1)} fusion(f32[1,2,512,240]{2,3,1,0:T(8,128)S(1)} %get-tuple-element.8), kind=kOutput, calls=%fused_computation.50 | convolution fusion | flops 1513619456 | bytes 1966080 | tf_op jit(solution)/shard_map/mk,jkc->jmc/dot_general | solution.py:70
  301.4 6.2 %convolution_add_fusion = f32[2,240,512]{2,1,0:T(8,128)S(1)} fusion(f32[2,240,512]{2,1,0:T(8,128)S(1)} %fusion.24, f32[1,2,512,240]{2,3,1,0:T(8,128)S(1)} %get-tuple-element.7), kind=kOutput, calls=%fused_computation.39 | convolution fusion | flops 1513865216 | bytes 2949120 | tf_op jit(solution)/shard_map/mk,jkc->jmc/dot_general | solution.py:73
  307.6 6.5 %subtract_bitcast_fusion.1 = (f32[1,2,512,240]{2,3,1,0:T(8,128)S(1)}, f32[1,2,512,240]{2,3,1,0:T(8,128)S(1)}) fusion(f32[2,240,512]{2,1,0:T(8,128)S(1)} %convolution_add_fusion, f32[2,512]{1,0:T(2,128)S(1)} %get-tuple-element.19, f32[2,512]{1,0:T(2,128)S(1)} %get-tuple-element.18, f32[2,240,512]{2,1,0:T(8,128)S(1)} %fusion.28, ...), kind=kOutput, calls=%fused_computation.73 | convolution fusion | flops 1515339776 | bytes 4923392 | tf_op jit(solution)/shard_map/mk,jkc->jmc/dot_general | solution.py:70
  314.1 1.5 pad_maximum_fusion.1
  315.6 2.9 copy.74
  318.5 55.5 %all_to_all.54 = f32[2,2,512,240]{3,1,0,2:T(2,128)S(1)} all-to-all(f32[2,2,512,240]{3,1,0,2:T(2,128)S(1)} %copy.74), channel_id=1, replica_groups=mesh['ctx'=64,'tp'=8] {'ctx'}, dimensions={2} | all-to-all | bytes 3932160 | tf_op jit(solution)/shard_map/all_to_all | solution.py:82
  374.0 0.4 copy.106
  374.4 0.1 fusion.149
  374.6 0.1 copy.76
  374.7 1.0 fusion.35
  375.8 0.1 copy.78
  375.9 1.1 fusion.20
  377.0 0.3 copy.80
  377.3 22.1 %all_to_all.55 = f32[64,8,240]{2,1,0:T(8,128)S(1)} all-to-all(f32[64,8,240]{2,1,0:T(8,128)S(1)} %copy.80), channel_id=1, replica_groups=mesh['ctx'=64,'tp'=8] {'ctx'}, dimensions={0} | all-to-all | bytes 983040 | tf_op jit(solution)/shard_map/all_to_all | solution.py:92
  399.4 0.2 copy.81
  399.6 4.0 convolution_bitcast_fusion
  403.6 5.5 %copy.88 = f32[1920,512]{1,0:T(8,128)} copy(f32[1920,512]{0,1:T(8,128)} %convolution_bitcast_fusion) | data formatting | bytes 7864320
  409.1 97.0 %reduce-scatter.4.cloned.1.call-done = f32[240,512]{1,0:T(8,128)} async-done(((f32[1920,512]{1,0:T(8,128)}), f32[240,512]{1,0:T(8,128)}) %reduce-scatter.4.cloned.1.call-update) | async-done | bytes 491536 | tf_op jit(solution)/shard_map/reduce_scatter | solution.py:137
  506.1 1.8 convert_element_type.88
  (27 shorter events, 0.5 us)
Async XLA Ops:
  6.5 70.8 %copy-start = (bf16[3,240,1920]{2,1,0:T(8,128)(2,1)S(1)}, bf16[3,240,1920]{2,1,0:T(8,128)(2,1)}, u32[]{:S(2)}) copy-start(bf16[3,240,1920]{2,1,0:T(8,128)(2,1)} %param.10) | copy-start | bytes 8294404
  6.5 68.6 %all-gather.2.cloned.1.call-start = ((), (), s32[]{:S(2)}) async-start(), calls=%async_computation.5 | async-start | bytes 2211840 | tf_op jit(solution)/shard_map/all_gather | solution.py:102
  8.1 69.2 %copy-start.7 = (f32[1920]{0:T(1024)S(1)}, f32[1920]{0:T(1024)}, u32[]{:S(2)}) copy-start(f32[1920]{0:T(1024)} %param.9) | copy-start | bytes 23044
  75.2 2.2 copy-start.3
  77.4 3.9 copy-start.5
  79.3 12.6 %collective-permute-start = (bf16[3,240,2]{2,1,0:T(8,128)(2,1)S(1)}, bf16[3,240,2]{2,1,0:T(8,128)(2,1)S(1)}, u32[]{:S(2)}, u32[]{:S(2)}) collective-permute-start(bf16[3,240,2]{2,1,0:T(8,128)(2,1)S(1)} %slice.74), channel_id=1, source_target_pairs={{0,8},{8,16},{16,24},{24,32},{32,40},{40,48},{48,56},{56,64},{64,7... | collective-permute-start | bytes 8648 | tf_op jit(solution)/shard_map/ppermute | solution.py:14
  93.5 1.2 copy-start.2
  96.2 31.9 %all-to-all-start = ((f32[2,1,512,240]{3,0,1,2:T(2,128)}), f32[2,1,512,240]{3,0,1,2:T(2,128)S(1)}, u32[]{:S(2)}, u32[]{:S(2)}) async-start(f32[2,1,512,240]{3,0,1,2:T(2,128)} %copy.65), calls=%async_computation | async-start | bytes 2097152 | tf_op jit(solution)/shard_map/all_to_all | solution.py:28
  142.6 100.6 %all-to-all-start.1 = ((f32[2,2,128,8,240]{4,3,0,1,2:T(8,128)}), f32[2,2,128,8,240]{4,3,0,1,2:T(8,128)}, u32[]{:S(2)}, u32[]{:S(2)}) async-start(f32[2,2,128,8,240]{4,3,0,1,2:T(8,128)} %copy.69), calls=%async_computation.1 | async-start | bytes 8388608 | tf_op jit(solution)/shard_map/all_to_all | solution.py:46
  150.1 356.0 %reduce-scatter.4.cloned.1.call-start = ((), (), s32[]{:S(2)}) async-start(), calls=%async_computation.6 | async-start | bytes 4423680 | tf_op jit(solution)/shard_map/reduce_scatter | solution.py:137
  377.0 22.6 %copy-start.6 = (f32[240]{0:T(256)S(1)}, f32[240]{0:T(256)}, u32[]{:S(2)}) copy-start(f32[240]{0:T(256)} %param.14) | copy-start | bytes 2884
  377.3 22.3 %copy-start.4 = (bf16[240,1920]{1,0:T(8,128)(2,1)S(1)}, bf16[240,1920]{1,0:T(8,128)(2,1)}, u32[]{:S(2)}) copy-start(bf16[240,1920]{1,0:T(8,128)(2,1)} %param.15) | copy-start | bytes 2764804
  409.1 98.7 %copy-start.1 = (bf16[3,240,1920]{2,1,0:T(8,128)(2,1)S(1)}, bf16[3,240,1920]{2,1,0:T(8,128)(2,1)}, u32[]{:S(2)}) copy-start(bf16[3,240,1920]{2,1,0:T(8,128)(2,1)} %param.10) | copy-start | bytes 8294404
Sparse Core Ops, SparseCore 0:
  9.5 65.6 all-gather.1
  409.3 96.7 reduce-scatter.3
where the time goes:
time: 521 us; the launch traced here: 515 us
  waiting for transfers between devices  293 us (56%)
  matrix products  82.6 us (16%)
  blocking collectives  77.6 us (15%)
  local copies, waits for them, and re-layouts  20.4 us (4%)
  starting transfers between devices  15.3 us (3%)
  between operations  14 us (3%)
  other arithmetic  12.5 us (2%)
    reduce_scatter x1, waiting for transfers between devices, body(): lax.psum_scatter(partial_terms, 'tp', scatter_dimension=0, tiled=True)  97 us
    all_to_all x1, waiting for transfers between devices, forward_spectrum(): lax.all_to_all(jnp.stack([real_second, imag_second], 1), 'ctx', split_axi...  92.6 us
    all_gather x1, waiting for transfers between devices, body(): lax.all_gather(tokens, 'tp', axis=0, tiled=True).astype(jnp.float32)  65.5 us
    all_to_all x1, blocking collectives, inverse_spectrum(): lax.all_to_all(jnp.stack([real_second, imag_second], 0), 'ctx', split_axi...  55.5 us
    all_to_all x1, waiting for transfers between devices, forward_spectrum(): lax.all_to_all(fields.reshape(count, 1, row_count, local_width), 'ctx', s...  26.2 us
    all_to_all x1, blocking collectives, inverse_spectrum(): lax.all_to_all(values, 'ctx', split_axis=0, concat_axis=1, tiled=True)  22.1 us
    dot_general x1, matrix products, forward_spectrum(): jnp.einsum('km,fjmc->fjkc', inner_sin, real_in, precision=highest)  10.8 us
    dot_general x1, matrix products, forward_spectrum(): jnp.einsum('km,fjmc->fjkc', inner_cos, imag_in, precision=highest)  10.8 us
  transfers between devices with their start and end apart: 5, of which 5 were waited for; matrix products, arithmetic and copies ran while one was open for 1% of the time, Pallas kernels for 0%

commit v1 on v0

v1 whole, which is shorter than its diff:
```python
import functools

import jax
import jax.numpy as jnp
from jax import lax
from jax.experimental import pallas as pl
from jax.experimental.pallas import tpu as pltpu
from jax.sharding import PartitionSpec as P

MESH = pl.DeviceIdType.MESH
F32 = jnp.float32
BF16 = jnp.bfloat16
RING = 4
LINE = 4
LANES = 128
SUBS = 8


def aligned(value, step):
    return pl.multiple_of(value, step)


def mixer_kernel(
    sizes,
    tokens,
    gain,
    w_in,
    w_short,
    decay,
    residue,
    skip,
    w_out,
    out,
    feat,
    win,
    gmat,
    norm,
    proj,
    sig,
    qry,
    gat,
    taps,
    rates,
    gains,
    skips,
    ends,
    starts,
    own_state,
    line_state,
    line_total,
    totals,
    wraw,
    wturn,
    wsib,
    gown,
    gsib,
    far_out,
    far_in,
    up_out,
    up_in,
    down_out,
    down_in,
    held,
    mine,
    local_sem,
    gather_send,
    gather_recv,
    halo_send,
    halo_recv,
    wsib_send,
    wsib_recv,
    line_send,
    line_recv,
    total_send,
    total_recv,
    gsib_send,
    gsib_recv,
    sum_send,
    sum_recv,
):
    part_count, line_count = sizes
    width, rows = tokens.shape
    depth = w_in.shape[2]
    chan = w_in.shape[1]
    wide = 2 * LANES
    chunks = rows // LANES
    low = LANES
    high = width - LANES
    modes = decay.shape[0]
    steps = rows // SUBS

    ctx = lax.axis_index("ctx")
    tp = lax.axis_index("tp")
    core = lax.rem(tp, 2)
    chip = lax.div(tp, 2)
    place = lax.rem(ctx, LINE)
    line = lax.div(ctx, LINE)
    chip_up = lax.rem(chip + 1, RING)
    chip_down = lax.rem(chip + RING - 1, RING)
    chip_far = lax.rem(chip + 2, RING)
    other = 1 - core
    up = (ctx, chip_up * 2 + core)
    down = (ctx, chip_down * 2 + core)
    sibling = (ctx, chip * 2 + other)

    def remote(src, dst, send, recv, device):
        return pltpu.make_async_remote_copy(
            src_ref=src,
            dst_ref=dst,
            send_sem=send,
            recv_sem=recv,
            device_id=device,
            device_id_type=MESH,
        )

    loads = [
        pltpu.make_async_copy(
            tokens, feat.at[pl.ds(aligned(tp * width, 16), width), :], local_sem.at[0]
        ),
        pltpu.make_async_copy(w_out, wraw.at[pl.ds(0, chan), :], local_sem.at[1]),
    ]
    for stream in range(3):
        loads.append(
            pltpu.make_async_copy(
                w_in.at[stream], win.at[stream, pl.ds(0, chan), :], local_sem.at[2 + stream]
            )
        )
    for load in loads:
        load.start()

    barrier = pltpu.get_barrier_semaphore()

    def greet(device):
        pl.semaphore_signal(barrier, inc=1, device_id=device, device_id_type=MESH)

    greet(up)
    greet(down)
    greet(sibling)
    for step in range(1, LINE):
        greet((line * LINE + lax.rem(place + step, LINE), tp))

    def greet_line(step, carry):
        greet((lax.rem(line + step, line_count) * LINE + place, tp))
        return carry

    lax.fori_loop(1, line_count, greet_line, 0)

    @pl.when(ctx > 0)
    def _():
        greet((ctx - 1, tp))

    @pl.when(ctx < part_count - 1)
    def _():
        greet((ctx + 1, tp))

    win[:, pl.ds(chan, wide - chan), :] = jnp.zeros((3, wide - chan, depth), BF16)
    taps[...] = jnp.zeros(taps.shape, F32)
    rates[...] = jnp.zeros(rates.shape, F32)
    gains[...] = jnp.zeros(gains.shape, F32)
    skips[...] = jnp.zeros(skips.shape, F32)
    rest = chan - LANES
    rates[pl.ds(0, modes), :] = decay[:, pl.ds(0, LANES)]
    rates[pl.ds(modes, modes), pl.ds(0, rest)] = decay[:, pl.ds(LANES, rest)]
    gains[pl.ds(0, modes), :] = residue[:, pl.ds(0, LANES)]
    gains[pl.ds(modes, modes), pl.ds(0, rest)] = residue[:, pl.ds(LANES, rest)]
    skips[pl.ds(0, 1), :] = skip[:, pl.ds(0, LANES)]
    skips[pl.ds(1, 1), pl.ds(0, rest)] = skip[:, pl.ds(LANES, rest)]
    for tap in range(3):
        for stream in range(3):
            row = tap * 3 + stream
            taps[pl.ds(row, 1), :] = w_short[tap, pl.ds(stream, 1), pl.ds(0, LANES)]
            taps[pl.ds(16 + row, 1), pl.ds(0, rest)] = w_short[
                tap, pl.ds(stream, 1), pl.ds(LANES, rest)
            ]
    bend = jnp.tanh(rates[...])
    gains[...] = gains[...] * jnp.sqrt(2.0 * bend / (1.0 + bend))

    wait_count = (
        3
        + (LINE - 1)
        + (line_count - 1)
        + jnp.where(ctx > 0, 1, 0)
        + jnp.where(ctx < part_count - 1, 1, 0)
    )
    pl.semaphore_wait(barrier, wait_count)

    def chunk_at(index):
        return lax.rem(index + chunks - 1, chunks)

    def block(chip_index, core_index, index, part):
        first, count = ((0, low), (low, high), (0, width))[part]
        start = (chip_index * 2 + core_index) * width + first
        return feat.at[
            pl.ds(aligned(start, 16), count),
            pl.ds(aligned(chunk_at(index) * LANES, LANES), LANES),
        ]

    def token_block(index, part):
        first, count = ((0, low), (low, high), (0, width))[part]
        return tokens.at[
            pl.ds(first, count), pl.ds(aligned(chunk_at(index) * LANES, LANES), LANES)
        ]

    def gather_copy(index, kind):
        sems = (gather_send.at[index, kind], gather_recv.at[index, kind])
        if kind < 4:
            part = kind % 2
            return remote(
                token_block(index, part),
                block(chip, core, index, part),
                *sems,
                up if kind < 2 else down,
            )
        if kind == 4:
            here = block(chip_down, core, index, 0)
            return remote(here, here, *sems, up)
        if kind == 5:
            here = block(chip_up, core, index, 1)
            return remote(here, here, *sems, down)
        if kind == 6:
            return remote(token_block(index, 2), block(chip, core, index, 2), *sems, sibling)
        whose = {7: chip_down, 8: chip_up, 9: chip_far}[kind]
        here = block(whose, core, index, 2)
        return remote(here, here, *sems, sibling)

    def gather_wait(index, kind):
        whose, owner, part = {
            0: (chip_down, core, 0),
            1: (chip_down, core, 1),
            2: (chip_up, core, 0),
            3: (chip_up, core, 1),
            4: (chip_far, core, 0),
            5: (chip_far, core, 1),
            6: (chip, other, 2),
            7: (chip_down, other, 2),
            8: (chip_up, other, 2),
            9: (chip_far, other, 2),
        }[kind]
        here = block(whose, owner, index, part)
        remote(
            here, here, gather_send.at[index, kind], gather_recv.at[index, kind], sibling
        ).wait_recv()

    def send_own(index, carry):
        for kind in (0, 3, 1, 2, 6):
            gather_copy(index, kind).start()
        return carry

    lax.fori_loop(0, chunks, send_own, 0)

    loads[1].wait()
    wraw[pl.ds(chan, wide - chan), :] = jnp.zeros((wide - chan, depth), BF16)

    def turn(index, carry):
        span = pl.ds(aligned(index * LANES, LANES), LANES)
        gmat[span, :] = jnp.broadcast_to(gain[:, span], (LANES, LANES)).T
        wturn[span, :] = wraw[:, span].astype(F32).T.astype(BF16)
        return carry

    lax.fori_loop(0, depth // LANES, turn, 0)

    def wsib_copy(index):
        return remote(
            wturn.at[pl.ds(aligned((index * 2 + other) * width, 16), width), :],
            wsib.at[pl.ds(index * width, width), :],
            wsib_send.at[index],
            wsib_recv.at[index],
            sibling,
        )

    for index in range(RING):
        wsib_copy(index).start()

    @pl.when(ctx == 0)
    def _():
        proj[:, pl.ds(0, SUBS), :] = jnp.zeros((6, SUBS, LANES), F32)

    def halo_copy():
        return remote(
            proj.at[:, pl.ds(rows, SUBS), :],
            proj.at[:, pl.ds(0, SUBS), :],
            halo_send.at[0],
            halo_recv.at[0],
            (jnp.minimum(ctx + 1, part_count - 1), tp),
        )

    def forward(index):
        gather_wait(index, 0)
        gather_copy(index, 4).start()
        gather_wait(index, 3)
        gather_copy(index, 5).start()

    def project(chunk):
        span = pl.ds(aligned(chunk * LANES, LANES), LANES)

        def square(index, total):
            value = feat[pl.ds(aligned(index * LANES, LANES), LANES), span].astype(F32)
            return total + jnp.sum((value * value).reshape(LANES // 8, 8, LANES), axis=0)

        total = lax.fori_loop(0, depth // LANES, square, jnp.zeros((8, LANES), F32))
        scale = lax.rsqrt(jnp.sum(total, axis=0, keepdims=True) / depth + 1e-06)

        def normalise(index, carry):
            here = pl.ds(aligned(index * LANES, LANES), LANES)
            value = feat[here, span].astype(F32)
            norm[here, :] = (value * scale * gmat[here, :]).astype(BF16)
            return carry

        lax.fori_loop(0, depth // LANES, normalise, 0)

        def stream_of(stream, carry):
            value = jnp.dot(win[stream], norm[...], preferred_element_type=F32)
            value = value.astype(BF16).astype(F32)
            target = pl.ds(aligned(SUBS + chunk * LANES, 8), LANES)
            for tile in range(2):
                proj[stream * 2 + tile, target, :] = value[tile * LANES : (tile + 1) * LANES].T
            return carry

        lax.fori_loop(0, 3, stream_of, 0)

    def short_mix(chunk):
        for tile in range(2):
            mixed = []
            for stream in range(3):
                piece = proj[
                    stream * 2 + tile, pl.ds(aligned(chunk * LANES, 8), LANES + SUBS), :
                ]
                value = taps[pl.ds(16 * tile + stream, 1), :] * piece[SUBS:]
                for tap in range(1, 3):
                    value = (
                        value
                        + taps[pl.ds(16 * tile + tap * 3 + stream, 1), :]
                        * piece[SUBS - tap : SUBS - tap + LANES]
                    )
                mixed.append(value)
            target = pl.ds(aligned(tile * rows + chunk * LANES, 8), LANES)
            qry[target, :] = mixed[0]
            sig[target, :] = mixed[1] * mixed[2]

    forward(0)
    for load in loads[2:]:
        load.wait()
    loads[0].wait()

    def take_chunk(index, carry):
        @pl.when(index < chunks - 1)
        def _():
            forward(index + 1)

        gather_wait(index, 1)
        gather_copy(index, 7).start()
        gather_wait(index, 2)
        gather_copy(index, 8).start()
        gather_wait(index, 4)
        gather_wait(index, 5)
        gather_copy(index, 9).start()
        for kind in (6, 7, 8, 9):
            gather_wait(index, kind)
        project(chunk_at(index))

        @pl.when((index == 0) & (ctx < part_count - 1))
        def _():
            halo_copy().start()

        @pl.when((index == 1) & (ctx > 0))
        def _():
            halo_copy().wait_recv()

        @pl.when(index > 0)
        def _():
            short_mix(chunk_at(index))

        return carry

    lax.fori_loop(0, chunks, take_chunk, 0)
    short_mix(chunks - 1)

    def advance(tile):
        keep = [
            jnp.broadcast_to(
                jnp.exp(-rates[pl.ds(tile * modes + mode, 1), :]), (SUBS, LANES)
            )
            for mode in range(modes)
        ]

        def step_of(step, states):
            value = sig[pl.ds(tile * rows + step, SUBS, stride=steps), :]
            return tuple(keep[mode] * states[mode] + value for mode in range(modes))

        states = lax.fori_loop(
            0, steps, step_of, tuple(jnp.zeros((SUBS, LANES), F32) for _ in range(modes)),
            unroll=4,
        )
        for mode in range(modes):
            ends[pl.ds((tile * modes + mode) * SUBS, SUBS), :] = states[mode]

    for tile in range(2):
        advance(tile)

    all_rates = rates[...]
    stretch_keep = jnp.exp(-all_rates * float(steps))
    block_keep = jnp.exp(-all_rates * float(rows))
    line_keep = jnp.exp(-all_rates * float(rows * LINE))

    def stretch_end(index):
        return ends[pl.ds(index, 2 * modes, stride=SUBS), :]

    state = stretch_end(0)
    for index in range(1, SUBS):
        state = stretch_keep * state + stretch_end(index)
    own_state[...] = state

    def line_copy(step):
        return remote(
            own_state,
            line_state.at[place],
            line_send.at[step],
            line_recv.at[place],
            (line * LINE + lax.rem(place + step, LINE), tp),
        )

    for step in range(1, LINE):
        line_copy(step).start()
    for step in range(1, LINE):
        source = lax.rem(place + step, LINE)
        remote(
            own_state, line_state.at[source], line_send.at[step], line_recv.at[source], sibling
        ).wait_recv()
    line_state[place] = state

    total = jnp.zeros(state.shape, F32)
    before = total
    for index in range(LINE):
        before = jnp.where(place == index, total, before)
        total = block_keep * total + line_state[index]
    line_total[...] = total

    def total_copy(step):
        return remote(
            line_total,
            totals.at[line],
            total_send.at[step],
            total_recv.at[line],
            (jnp.minimum(line + step, line_count - 1) * LINE + place, tp),
        )

    def total_start(step, carry):
        total_copy(step).start()
        return carry

    lax.fori_loop(1, line_count - line, total_start, 0)

    def total_take(index, value):
        remote(
            line_total, totals.at[index], total_send.at[0], total_recv.at[index], sibling
        ).wait_recv()
        return line_keep * value + totals[index]

    entering = lax.fori_loop(0, line, total_take, jnp.zeros(state.shape, F32))
    state = jnp.exp(-all_rates * (place * rows).astype(F32)) * entering + before
    for index in range(SUBS):
        starts[pl.ds(index * 2 * modes, 2 * modes), :] = state
        state = stretch_keep * state + stretch_end(index)

    def emit(tile):
        keep = [
            jnp.broadcast_to(
                jnp.exp(-rates[pl.ds(tile * modes + mode, 1), :]), (SUBS, LANES)
            )
            for mode in range(modes)
        ]
        scale = [
            jnp.broadcast_to(gains[pl.ds(tile * modes + mode, 1), :], (SUBS, LANES))
            for mode in range(modes)
        ]
        direct = jnp.broadcast_to(skips[pl.ds(tile, 1), :], (SUBS, LANES))

        def step_of(step, states):
            span = pl.ds(tile * rows + step, SUBS, stride=steps)
            value = sig[span, :]
            states = tuple(keep[mode] * states[mode] + value for mode in range(modes))
            terms = [scale[mode] * states[mode] for mode in range(modes)]
            while len(terms) > 1:
                terms = [terms[k] + terms[k + 1] for k in range(0, len(terms), 2)]
            gat[span, :] = qry[span, :] * (terms[0] + direct * value)
            return states

        first = tuple(
            starts[pl.ds(tile * modes + mode, SUBS, stride=2 * modes), :]
            for mode in range(modes)
        )
        lax.fori_loop(0, steps, step_of, first, unroll=2)

    for tile in range(2):
        emit(tile)

    def gsib_copy(chunk):
        span = pl.ds(aligned(chunk * LANES, LANES), LANES)
        return remote(
            gown.at[span, :], gsib.at[span, :], gsib_send.at[chunk], gsib_recv.at[chunk], sibling
        )

    def share(chunk, carry):
        span = pl.ds(aligned(chunk * LANES, LANES), LANES)
        for tile in range(2):
            gown[span, pl.ds(tile * LANES, LANES)] = gat[
                pl.ds(aligned(tile * rows + chunk * LANES, LANES), LANES), :
            ].astype(BF16)
        gsib_copy(chunk).start()
        return carry

    lax.fori_loop(0, chunks, share, 0)
    for index in range(RING):
        remote(
            wturn.at[pl.ds(0, width), :],
            wsib.at[pl.ds(index * width, width), :],
            wsib_send.at[index],
            wsib_recv.at[index],
            sibling,
        ).wait_recv()

    def partial(target, chunk):
        span = pl.ds(aligned(chunk * LANES, LANES), LANES)
        dims = (((1,), (1,)), ((), ()))
        value = lax.dot_general(
            wturn[pl.ds(aligned((target * 2 + core) * width, 16), width), :],
            gown[span, :],
            dims,
            preferred_element_type=F32,
        )
        return value + lax.dot_general(
            wsib[pl.ds(aligned(target * width, 16), width), :],
            gsib[span, :],
            dims,
            preferred_element_type=F32,
        )

    lower, upper = pl.ds(0, low), pl.ds(low, high)

    def sum_copy(chunk, kind):
        source, target, part, device = (
            (far_out, far_in, lower, up),
            (far_out, far_in, upper, down),
            (up_out, up_in, upper, up),
            (down_out, down_in, lower, down),
            (up_out, up_in, lower, up),
            (down_out, down_in, upper, down),
        )[kind]
        return remote(
            source.at[chunk, part, :],
            target.at[chunk, part, :],
            sum_send.at[chunk, kind],
            sum_recv.at[chunk, kind],
            device,
        )

    def send_far(chunk, carry):
        gsib_copy(chunk).wait_recv()
        far_out[chunk] = partial(chip_far, chunk).astype(BF16)
        sum_copy(chunk, 0).start()
        sum_copy(chunk, 1).start()
        return carry

    lax.fori_loop(0, chunks, send_far, 0)

    def send_near(chunk, carry):
        value = partial(chip_up, chunk)
        up_out[chunk, upper, :] = value[low:].astype(BF16)
        sum_copy(chunk, 2).start()
        held[chunk, lower, :] = value[:low]
        value = partial(chip_down, chunk)
        down_out[chunk, lower, :] = value[:low].astype(BF16)
        sum_copy(chunk, 3).start()
        held[chunk, upper, :] = value[low:]
        return carry

    lax.fori_loop(0, chunks, send_near, 0)

    def send_sums(chunk, carry):
        sum_copy(chunk, 0).wait_recv()
        up_out[chunk, lower, :] = (
            held[chunk, lower, :] + far_in[chunk, lower, :].astype(F32)
        ).astype(BF16)
        sum_copy(chunk, 4).start()
        sum_copy(chunk, 1).wait_recv()
        down_out[chunk, upper, :] = (
            held[chunk, upper, :] + far_in[chunk, upper, :].astype(F32)
        ).astype(BF16)
        sum_copy(chunk, 5).start()
        mine[chunk] = partial(chip, chunk)
        return carry

    lax.fori_loop(0, chunks, send_sums, 0)

    def finish(chunk, carry):
        for kind in range(2, 6):
            sum_copy(chunk, kind).wait_recv()
        value = mine[chunk] + up_in[chunk].astype(F32) + down_in[chunk].astype(F32)
        out[:, pl.ds(aligned(chunk * LANES, LANES), LANES)] = value.astype(BF16)
        return carry

    lax.fori_loop(0, chunks, finish, 0)

    def drain(index, carry):
        for kind in range(10):
            gather_copy(index, kind).wait_send()
        for kind in range(6):
            sum_copy(index, kind).wait_send()
        gsib_copy(index).wait_send()
        return carry

    lax.fori_loop(0, chunks, drain, 0)
    for index in range(RING):
        wsib_copy(index).wait_send()
    for step in range(1, LINE):
        line_copy(step).wait_send()

    def total_drain(step, carry):
        total_copy(step).wait_send()
        return carry

    lax.fori_loop(1, line_count - line, total_drain, 0)

    @pl.when(ctx < part_count - 1)
    def _():
        halo_copy().wait_send()


def solution(mesh):
    part_count = mesh.shape["ctx"]
    line_count = part_count // LINE

    def body(tokens, norm_gain, w_in, w_short, decay_rate, residue, skip_gain, w_out):
        width, rows = tokens.shape
        chan, depth = w_in.shape[1:]
        modes = decay_rate.shape[0]
        chunks = rows // LANES
        wide = 2 * LANES
        vmem = pltpu.VMEM
        dma = pltpu.SemaphoreType.DMA
        hbm = pl.BlockSpec(memory_space=pl.ANY)
        near = pl.BlockSpec(memory_space=pltpu.VMEM)
        scratch = [
            vmem((depth, rows), BF16),
            vmem((3, wide, depth), BF16),
            vmem((depth, LANES), F32),
            vmem((depth, LANES), BF16),
            vmem((6, SUBS + rows, LANES), F32),
            vmem((2 * rows, LANES), F32),
            vmem((2 * rows, LANES), F32),
            vmem((2 * rows, LANES), F32),
            vmem((32, LANES), F32),
            vmem((2 * modes, LANES), F32),
            vmem((2 * modes, LANES), F32),
            vmem((8, LANES), F32),
            vmem((2 * modes * SUBS, LANES), F32),
            vmem((2 * modes * SUBS, LANES), F32),
            vmem((2 * modes, LANES), F32),
            vmem((LINE, 2 * modes, LANES), F32),
            vmem((2 * modes, LANES), F32),
            vmem((line_count, 2 * modes, LANES), F32),
            vmem((wide, depth), BF16),
            vmem((depth, wide), BF16),
            vmem((RING * width, wide), BF16),
            vmem((rows, wide), BF16),
            vmem((rows, wide), BF16),
            vmem((chunks, width, LANES), BF16),
            vmem((chunks, width, LANES), BF16),
            vmem((chunks, width, LANES), BF16),
            vmem((chunks, width, LANES), BF16),
            vmem((chunks, width, LANES), BF16),
            vmem((chunks, width, LANES), BF16),
            vmem((chunks, width, LANES), F32),
            vmem((chunks, width, LANES), F32),
            dma((5,)),
            dma((chunks, 10)),
            dma((chunks, 10)),
            dma((1,)),
            dma((1,)),
            dma((RING,)),
            dma((RING,)),
            dma((LINE,)),
            dma((LINE,)),
            dma((line_count,)),
            dma((line_count,)),
            dma((chunks,)),
            dma((chunks,)),
            dma((chunks, 6)),
            dma((chunks, 6)),
        ]
        return pl.pallas_call(
            functools.partial(mixer_kernel, (part_count, line_count)),
            out_shape=jax.ShapeDtypeStruct((width, rows), BF16),
            in_specs=[hbm, near, hbm, near, near, near, near, hbm],
            out_specs=near,
            scratch_shapes=scratch,
            compiler_params=pltpu.CompilerParams(collective_id=0, has_side_effects=True),
        )(
            tokens,
            norm_gain[None, :],
            w_in,
            w_short,
            decay_rate,
            residue,
            skip_gain[None, :],
            w_out,
        )

    placed = (
        P("tp", "ctx"),
        P(),
        P(None, "tp", None),
        P(None, None, "tp"),
        P(None, "tp"),
        P(None, "tp"),
        P("tp"),
        P("tp", None),
    )
    return jax.shard_map(
        body, mesh=mesh, in_specs=placed, out_specs=P("tp", "ctx"), check_vma=False
    )
```

time: 521 us -> 116 us (0.22)
  the two profiles are of different devices: /device:TPU:25 before, /device:TPU:29 now
where the time goes in v1:
time: 116 us; the launch traced here: 115 us
  Pallas kernels  112 us (97%)
  local copies, waits for them, and re-layouts  2.95 us (3%)
    pallas_call x1, Pallas kernels, body(): pl.pallas_call(functools.partial(mixer_kernel, (part_count, line_count)),...  112 us

profile of v1, /device:TPU:29, one launch (start us, length us, event | category | flops | bytes accessed | tf_op | source)
XLA Modules:
  0.0 115.4 jit_solution(13333917529690862102)
XLA Ops:
  0.0 1.3 %broadcast_in_dim.6.gain = f32[1,1920]{1,0:T(1,128)} reshape(f32[1920]{0:T(1024)} %param.9) | data formatting | bytes 15360 | tf_op jit(solution)/shard_map/broadcast_in_dim | solution.py:700
  1.3 112.4 %shard_map.82 = bf16[240,512]{1,0:T(8,128)(2,1)} custom-call(bf16[240,512]{1,0:T(8,128)(2,1)} %tokens.1, f32[1,1920]{1,0:T(1,128)} %broadcast_in_dim.6.gain, bf16[3,240,1920]{2,1,0:T(8,128)(2,1)} %w_in.1, f32[3,3,240]{2,1,0:T(4,128)} %w_short.1, f32[16,240]{1,0:T(8,128)} %decay.1, f32[16,240]{1,0:T(8,128)} %residue.1, f32[1,240]{1,0:T(1,128)} %bitcast.1, ...), custom_call_target="tpu_custom_call" | custom-call | tf_op jit(solution)/shard_map/pallas_call | solution.py:691
  113.7 1.7 %copy.10 = bf16[240,512]{1,0:T(8,128)(2,1)} copy(bf16[240,512]{1,0:T(8,128)(2,1)} %shard_map.82) | data formatting | bytes 491520

commit v2 on v1

--- a/solution.py
+++ b/solution.py
@@ -23,14 +23,19 @@
 def mixer_kernel(
     sizes,
     tokens,
+    gain_ref,
+    w_in,
+    short_ref,
+    decay_ref,
+    residue_ref,
+    skip_ref,
+    w_out,
+    out,
     gain,
-    w_in,
     w_short,
     decay,
     residue,
     skip,
-    w_out,
-    out,
     feat,
     win,
     gmat,
@@ -45,6 +50,12 @@
     skips,
     ends,
     starts,
+    lead,
+    keep_one,
+    keep_eight,
+    wide_gain,
+    chunk_end,
+    enter,
     own_state,
     line_state,
     line_total,
@@ -86,8 +97,8 @@
     chunks = rows // LANES
     low = LANES
     high = width - LANES
-    modes = decay.shape[0]
-    steps = rows // SUBS
+    modes = decay_ref.shape[0]
+    steps = LANES // SUBS
 
     ctx = lax.axis_index("ctx")
     tp = lax.axis_index("tp")
@@ -113,6 +124,31 @@
             device_id_type=MESH,
         )
 
+    barrier = pltpu.get_barrier_semaphore()
+
+    def greet(device):
+        pl.semaphore_signal(barrier, inc=1, device_id=device, device_id_type=MESH)
+
+    greet(up)
+    greet(down)
+    greet(sibling)
+    for step in range(1, LINE):
+        greet((line * LINE + lax.rem(place + step, LINE), tp))
+
+    def greet_line(step, carry):
+        greet((lax.rem(line + step, line_count) * LINE + place, tp))
+        return carry
+
+    lax.fori_loop(1, line_count, greet_line, 0)
+
+    @pl.when(ctx > 0)
+    def _():
+        greet((ctx - 1, tp))
+
+    @pl.when(ctx < part_count - 1)
+    def _():
+        greet((ctx + 1, tp))
+
     loads = [
         pltpu.make_async_copy(
             tokens, feat.at[pl.ds(aligned(tp * width, 16), width), :], local_sem.at[0]
@@ -122,43 +158,33 @@
     for stream in range(3):
         loads.append(
             pltpu.make_async_copy(
-                w_in.at[stream], win.at[stream, pl.ds(0, chan), :], local_sem.at[2 + stream]
+                w_in.at[stream], win.at[pl.ds(stream * wide, chan), :], local_sem.at[2 + stream]
             )
         )
-    for load in loads:
+    small = [
+        pltpu.make_async_copy(source, target, local_sem.at[5 + index])
+        for index, (source, target) in enumerate(
+            (
+                (decay_ref, decay),
+                (residue_ref, residue),
+                (short_ref, w_short),
+                (skip_ref, skip),
+                (gain_ref, gain),
+            )
+        )
+    ]
+    for load in small + loads:
         load.start()
 
-    barrier = pltpu.get_barrier_semaphore()
-
-    def greet(device):
-        pl.semaphore_signal(barrier, inc=1, device_id=device, device_id_type=MESH)
-
-    greet(up)
-    greet(down)
-    greet(sibling)
-    for step in range(1, LINE):
-        greet((line * LINE + lax.rem(place + step, LINE), tp))
-
-    def greet_line(step, carry):
-        greet((lax.rem(line + step, line_count) * LINE + place, tp))
-        return carry
-
-    lax.fori_loop(1, line_count, greet_line, 0)
-
-    @pl.when(ctx > 0)
-    def _():
-        greet((ctx - 1, tp))
-
-    @pl.when(ctx < part_count - 1)
-    def _():
-        greet((ctx + 1, tp))
-
-    win[:, pl.ds(chan, wide - chan), :] = jnp.zeros((3, wide - chan, depth), BF16)
+    for stream in range(3):
+        win[pl.ds(stream * wide + chan, wide - chan), :] = jnp.zeros((wide - chan, depth), BF16)
     taps[...] = jnp.zeros(taps.shape, F32)
     rates[...] = jnp.zeros(rates.shape, F32)
     gains[...] = jnp.zeros(gains.shape, F32)
     skips[...] = jnp.zeros(skips.shape, F32)
     rest = chan - LANES
+    for load in small:
+        load.wait()
     rates[pl.ds(0, modes), :] = decay[:, pl.ds(0, LANES)]
     rates[pl.ds(modes, modes), pl.ds(0, rest)] = decay[:, pl.ds(LANES, rest)]
     gains[pl.ds(0, modes), :] = residue[:, pl.ds(0, LANES)]
@@ -242,18 +268,29 @@
         ).wait_recv()
 
     def send_own(index, carry):
-        for kind in (0, 3, 1, 2, 6):
+        for kind in (0, 3):
             gather_copy(index, kind).start()
         return carry
 
+    def send_rest(index, carry):
+        for kind in (1, 2):
+            gather_copy(index, kind).start()
+        return carry
+
+    def send_sibling(index, carry):
+        gather_copy(index, 6).start()
+        return carry
+
     lax.fori_loop(0, chunks, send_own, 0)
+    send_rest(0, 0)
+    lax.fori_loop(0, chunks, send_sibling, 0)
 
     loads[1].wait()
     wraw[pl.ds(chan, wide - chan), :] = jnp.zeros((wide - chan, depth), BF16)
 
     def turn(index, carry):
         span = pl.ds(aligned(index * LANES, LANES), LANES)
-        gmat[span, :] = jnp.broadcast_to(gain[:, span], (LANES, LANES)).T
+        gmat[span, :] = jnp.broadcast_to(gain[pl.ds(index, 1), :], (LANES, LANES)).T
         wturn[span, :] = wraw[:, span].astype(F32).T.astype(BF16)
         return carry
 
@@ -308,15 +345,11 @@
 
         lax.fori_loop(0, depth // LANES, normalise, 0)
 
-        def stream_of(stream, carry):
-            value = jnp.dot(win[stream], norm[...], preferred_element_type=F32)
-            value = value.astype(BF16).astype(F32)
-            target = pl.ds(aligned(SUBS + chunk * LANES, 8), LANES)
-            for tile in range(2):
-                proj[stream * 2 + tile, target, :] = value[tile * LANES : (tile + 1) * LANES].T
-            return carry
-
-        lax.fori_loop(0, 3, stream_of, 0)
+        value = jnp.dot(win[...], norm[...], preferred_element_type=F32)
+        value = value.astype(BF16).astype(F32)
+        target = pl.ds(aligned(SUBS + chunk * LANES, 8), LANES)
+        for tile in range(6):
+            proj[tile, target, :] = value[tile * LANES : (tile + 1) * LANES].T
 
     def short_mix(chunk):
         for tile in range(2):
@@ -337,179 +370,9 @@
             qry[target, :] = mixed[0]
             sig[target, :] = mixed[1] * mixed[2]
 
-    forward(0)
     for load in loads[2:]:
         load.wait()
     loads[0].wait()
-
-    def take_chunk(index, carry):
-        @pl.when(index < chunks - 1)
-        def _():
-            forward(index + 1)
-
-        gather_wait(index, 1)
-        gather_copy(index, 7).start()
-        gather_wait(index, 2)
-        gather_copy(index, 8).start()
-        gather_wait(index, 4)
-        gather_wait(index, 5)
-        gather_copy(index, 9).start()
-        for kind in (6, 7, 8, 9):
-            gather_wait(index, kind)
-        project(chunk_at(index))
-
-        @pl.when((index == 0) & (ctx < part_count - 1))
-        def _():
-            halo_copy().start()
-
-        @pl.when((index == 1) & (ctx > 0))
-        def _():
-            halo_copy().wait_recv()
-
-        @pl.when(index > 0)
-        def _():
-            short_mix(chunk_at(index))
-
-        return carry
-
-    lax.fori_loop(0, chunks, take_chunk, 0)
-    short_mix(chunks - 1)
-
-    def advance(tile):
-        keep = [
-            jnp.broadcast_to(
-                jnp.exp(-rates[pl.ds(tile * modes + mode, 1), :]), (SUBS, LANES)
-            )
-            for mode in range(modes)
-        ]
-
-        def step_of(step, states):
-            value = sig[pl.ds(tile * rows + step, SUBS, stride=steps), :]
-            return tuple(keep[mode] * states[mode] + value for mode in range(modes))
-
-        states = lax.fori_loop(
-            0, steps, step_of, tuple(jnp.zeros((SUBS, LANES), F32) for _ in range(modes)),
-            unroll=4,
-        )
-        for mode in range(modes):
-            ends[pl.ds((tile * modes + mode) * SUBS, SUBS), :] = states[mode]
-
-    for tile in range(2):
-        advance(tile)
-
-    all_rates = rates[...]
-    stretch_keep = jnp.exp(-all_rates * float(steps))
-    block_keep = jnp.exp(-all_rates * float(rows))
-    line_keep = jnp.exp(-all_rates * float(rows * LINE))
-
-    def stretch_end(index):
-        return ends[pl.ds(index, 2 * modes, stride=SUBS), :]
-
-    state = stretch_end(0)
-    for index in range(1, SUBS):
-        state = stretch_keep * state + stretch_end(index)
-    own_state[...] = state
-
-    def line_copy(step):
-        return remote(
-            own_state,
-            line_state.at[place],
-            line_send.at[step],
-            line_recv.at[place],
-            (line * LINE + lax.rem(place + step, LINE), tp),
-        )
-
-    for step in range(1, LINE):
-        line_copy(step).start()
-    for step in range(1, LINE):
-        source = lax.rem(place + step, LINE)
-        remote(
-            own_state, line_state.at[source], line_send.at[step], line_recv.at[source], sibling
-        ).wait_recv()
-    line_state[place] = state
-
-    total = jnp.zeros(state.shape, F32)
-    before = total
-    for index in range(LINE):
-        before = jnp.where(place == index, total, before)
-        total = block_keep * total + line_state[index]
-    line_total[...] = total
-
-    def total_copy(step):
-        return remote(
-            line_total,
-            totals.at[line],
-            total_send.at[step],
-            total_recv.at[line],
-            (jnp.minimum(line + step, line_count - 1) * LINE + place, tp),
-        )
-
-    def total_start(step, carry):
-        total_copy(step).start()
-        return carry
-
-    lax.fori_loop(1, line_count - line, total_start, 0)
-
-    def total_take(index, value):
-        remote(
-            line_total, totals.at[index], total_send.at[0], total_recv.at[index], sibling
-        ).wait_recv()
-        return line_keep * value + totals[index]
-
-    entering = lax.fori_loop(0, line, total_take, jnp.zeros(state.shape, F32))
-    state = jnp.exp(-all_rates * (place * rows).astype(F32)) * entering + before
-    for index in range(SUBS):
-        starts[pl.ds(index * 2 * modes, 2 * modes), :] = state
-        state = stretch_keep * state + stretch_end(index)
-
-    def emit(tile):
-        keep = [
-            jnp.broadcast_to(
-                jnp.exp(-rates[pl.ds(tile * modes + mode, 1), :]), (SUBS, LANES)
-            )
-            for mode in range(modes)
-        ]
-        scale = [
-            jnp.broadcast_to(gains[pl.ds(tile * modes + mode, 1), :], (SUBS, LANES))
-            for mode in range(modes)
-        ]
-        direct = jnp.broadcast_to(skips[pl.ds(tile, 1), :], (SUBS, LANES))
-
-        def step_of(step, states):
-            span = pl.ds(tile * rows + step, SUBS, stride=steps)
-            value = sig[span, :]
-            states = tuple(keep[mode] * states[mode] + value for mode in range(modes))
-            terms = [scale[mode] * states[mode] for mode in range(modes)]
-            while len(terms) > 1:
-                terms = [terms[k] + terms[k + 1] for k in range(0, len(terms), 2)]
-            gat[span, :] = qry[span, :] * (terms[0] + direct * value)
-            return states
-
-        first = tuple(
-            starts[pl.ds(tile * modes + mode, SUBS, stride=2 * modes), :]
-            for mode in range(modes)
-        )
-        lax.fori_loop(0, steps, step_of, first, unroll=2)
-
-    for tile in range(2):
-        emit(tile)
-
-    def gsib_copy(chunk):
-        span = pl.ds(aligned(chunk * LANES, LANES), LANES)
-        return remote(
-            gown.at[span, :], gsib.at[span, :], gsib_send.at[chunk], gsib_recv.at[chunk], sibling
-        )
-
-    def share(chunk, carry):
-        span = pl.ds(aligned(chunk * LANES, LANES), LANES)
-        for tile in range(2):
-            gown[span, pl.ds(tile * LANES, LANES)] = gat[
-                pl.ds(aligned(tile * rows + chunk * LANES, LANES), LANES), :
-            ].astype(BF16)
-        gsib_copy(chunk).start()
-        return carry
-
-    lax.fori_loop(0, chunks, share, 0)
     for index in range(RING):
         remote(
             wturn.at[pl.ds(0, width), :],
@@ -518,6 +381,211 @@
             wsib_recv.at[index],
             sibling,
         ).wait_recv()
+    ahead = (lax.broadcasted_iota(jnp.int32, (SUBS, LANES), 0) + 1).astype(F32)
+    for row in range(2 * modes):
+        span = pl.ds(row * SUBS, SUBS)
+        rate = jnp.broadcast_to(rates[pl.ds(row, 1), :], (SUBS, LANES))
+        wide_gain[span, :] = jnp.broadcast_to(gains[pl.ds(row, 1), :], (SUBS, LANES))
+        lead[span, :] = wide_gain[span, :] * jnp.exp(-rate * ahead)
+        keep_one[span, :] = jnp.exp(-rate)
+        keep_eight[span, :] = jnp.exp(-rate * float(SUBS))
+
+    all_rates = rates[...]
+    stretch_keep = jnp.exp(-all_rates * float(steps))
+    chunk_keep = jnp.exp(-all_rates * float(LANES))
+    block_keep = jnp.exp(-all_rates * float(rows))
+    line_keep = jnp.exp(-all_rates * float(rows * LINE))
+
+    def mode_rows(tile):
+        return [pl.ds((tile * modes + mode) * SUBS, SUBS) for mode in range(modes)]
+
+    def advance(chunk):
+        for tile in range(2):
+            spans = mode_rows(tile)
+            keep = [keep_one[span, :] for span in spans]
+
+            def step_of(step, states):
+                value = sig[pl.ds(tile * rows + chunk * LANES + step, SUBS, stride=steps), :]
+                return tuple(keep[mode] * states[mode] + value for mode in range(modes))
+
+            states = lax.fori_loop(
+                0,
+                steps,
+                step_of,
+                tuple(jnp.zeros((SUBS, LANES), F32) for _ in range(modes)),
+                unroll=4,
+            )
+            for span, state in zip(spans, states):
+                ends[span, :] = state
+        inner = jnp.zeros((2 * modes, LANES), F32)
+        for index in range(SUBS):
+            starts[chunk, pl.ds(index * 2 * modes, 2 * modes), :] = inner
+            inner = stretch_keep * inner + ends[pl.ds(index, 2 * modes, stride=SUBS), :]
+        chunk_end[chunk] = inner
+
+    def emit(chunk, carry):
+        for tile in range(2):
+            spans = mode_rows(tile)
+            keep = [keep_one[span, :] for span in spans]
+            scale = [wide_gain[span, :] for span in spans]
+            direct = jnp.broadcast_to(skips[pl.ds(tile, 1), :], (SUBS, LANES))
+
+            def step_of(step, states):
+                span = pl.ds(tile * rows + chunk * LANES + step, SUBS, stride=steps)
+                value = sig[span, :]
+                states = tuple(keep[mode] * states[mode] + value for mode in range(modes))
+                terms = [scale[mode] * states[mode] for mode in range(modes)]
+                while len(terms) > 1:
+                    terms = [terms[k] + terms[k + 1] for k in range(0, len(terms), 2)]
+                gat[span, :] = terms[0] + direct * value
+                return states
+
+            first = tuple(
+                starts[chunk, pl.ds(tile * modes + mode, SUBS, stride=2 * modes), :]
+                for mode in range(modes)
+            )
+            lax.fori_loop(0, steps, step_of, first, unroll=2)
+        return carry
+
+    def pass_near(index, carry):
+        gather_wait(index, 1)
+        gather_copy(index, 7).start()
+        gather_wait(index, 2)
+        gather_copy(index, 8).start()
+        return carry
+
+    def take_far(index):
+        gather_wait(index, 4)
+        gather_wait(index, 5)
+        gather_copy(index, 9).start()
+        for kind in (6, 7, 8, 9):
+            gather_wait(index, kind)
+        project(chunk_at(index))
+
+    forward(0)
+    send_rest(1, 0)
+    forward(1)
+    send_rest(2, 0)
+    send_rest(3, 0)
+    forward(2)
+    pass_near(0, 0)
+    take_far(0)
+
+    @pl.when(ctx < part_count - 1)
+    def _():
+        halo_copy().start()
+
+    forward(3)
+    lax.fori_loop(1, chunks, pass_near, 0)
+
+    def take_chunk(index, carry):
+        take_far(index)
+
+        @pl.when((index == 1) & (ctx > 0))
+        def _():
+            halo_copy().wait_recv()
+
+        short_mix(chunk_at(index))
+        advance(chunk_at(index))
+        return carry
+
+    lax.fori_loop(1, chunks, take_chunk, 0)
+    short_mix(chunks - 1)
+    advance(chunks - 1)
+
+    state = chunk_end[0]
+    for chunk in range(1, chunks):
+        state = chunk_keep * state + chunk_end[chunk]
+    own_state[...] = state
+
+    def line_copy(step):
+        return remote(
+            own_state,
+            line_state.at[place],
+            line_send.at[step],
+            line_recv.at[place],
+            (line * LINE + lax.rem(place + step, LINE), tp),
+        )
+
+    for step in range(1, LINE):
+        line_copy(step).start()
+
+    lax.fori_loop(0, 2, emit, 0)
+    for step in range(1, LINE):
+        source = lax.rem(place + step, LINE)
+        remote(
+            own_state, line_state.at[source], line_send.at[step], line_recv.at[source], sibling
+        ).wait_recv()
+    line_state[place] = state
+
+    total = jnp.zeros(state.shape, F32)
+    before = total
+    for index in range(LINE):
+        before = jnp.where(place == index, total, before)
+        total = block_keep * total + line_state[index]
+    line_total[...] = total
+
+    def total_copy(step):
+        return remote(
+            line_total,
+            totals.at[line],
+            total_send.at[step],
+            total_recv.at[line],
+            (jnp.minimum(line + step, line_count - 1) * LINE + place, tp),
+        )
+
+    def total_start(step, carry):
+        total_copy(step).start()
+        return carry
+
+    lax.fori_loop(1, line_count - line, total_start, 0)
+    lax.fori_loop(2, chunks, emit, 0)
+
+    def total_take(index, value):
+        remote(
+            line_total, totals.at[index], total_send.at[0], total_recv.at[index], sibling
+        ).wait_recv()
+        return line_keep * value + totals[index]
+
+    entering = lax.fori_loop(0, line, total_take, jnp.zeros(state.shape, F32))
+    state = jnp.exp(-all_rates * (place * rows).astype(F32)) * entering + before
+    for chunk in range(chunks):
+        enter[chunk] = state
+        state = chunk_keep * state + chunk_end[chunk]
+
+    def complete(chunk, tile):
+        spans = mode_rows(tile)
+        keep = [keep_eight[span, :] for span in spans]
+        base = chunk * LANES
+
+        def step_of(step, values):
+            halves = []
+            for half in range(2):
+                terms = list(values)
+                while len(terms) > 1:
+                    terms = [terms[k] + terms[k + 1] for k in range(0, len(terms), 2)]
+                span = pl.ds(
+                    aligned(tile * rows + base + step * 2 * SUBS + half * SUBS, SUBS), SUBS
+                )
+                halves.append(qry[span, :] * (gat[span, :] + terms[0]))
+                values = tuple(keep[mode] * values[mode] for mode in range(modes))
+            gown[
+                pl.ds(aligned(base + step * 2 * SUBS, 2 * SUBS), 2 * SUBS),
+                pl.ds(tile * LANES, LANES),
+            ] = jnp.concatenate(halves, axis=0).astype(BF16)
+            return values
+
+        values = tuple(
+            lead[spans[mode], :] * enter[chunk, pl.ds(tile * modes + mode, 1), :]
+            for mode in range(modes)
+        )
+        lax.fori_loop(0, LANES // (2 * SUBS), step_of, values)
+
+    def gsib_copy(chunk):
+        span = pl.ds(aligned(chunk * LANES, LANES), LANES)
+        return remote(
+            gown.at[span, :], gsib.at[span, :], gsib_send.at[chunk], gsib_recv.at[chunk], sibling
+        )
 
     def partial(target, chunk):
         span = pl.ds(aligned(chunk * LANES, LANES), LANES)
@@ -561,7 +629,19 @@
         sum_copy(chunk, 1).start()
         return carry
 
-    lax.fori_loop(0, chunks, send_far, 0)
+    def share(chunk, carry):
+        for tile in range(2):
+            complete(chunk, tile)
+        gsib_copy(chunk).start()
+
+        @pl.when(chunk > 0)
+        def _():
+            send_far(chunk - 1, 0)
+
+        return carry
+
+    lax.fori_loop(0, chunks, share, 0)
+    send_far(chunks - 1, 0)
 
     def send_near(chunk, carry):
         value = partial(chip_up, chunk)
@@ -641,8 +721,13 @@
         hbm = pl.BlockSpec(memory_space=pl.ANY)
         near = pl.BlockSpec(memory_space=pltpu.VMEM)
         scratch = [
+            vmem((depth // LANES, LANES), F32),
+            vmem(w_short.shape, F32),
+            vmem(decay_rate.shape, F32),
+            vmem(residue.shape, F32),
+            vmem((1, chan), F32),
             vmem((depth, rows), BF16),
-            vmem((3, wide, depth), BF16),
+            vmem((3 * wide, depth), BF16),
             vmem((depth, LANES), F32),
             vmem((depth, LANES), BF16),
             vmem((6, SUBS + rows, LANES), F32),
@@ -654,7 +739,13 @@
             vmem((2 * modes, LANES), F32),
             vmem((8, LANES), F32),
             vmem((2 * modes * SUBS, LANES), F32),
+            vmem((chunks, 2 * modes * SUBS, LANES), F32),
             vmem((2 * modes * SUBS, LANES), F32),
+            vmem((2 * modes * SUBS, LANES), F32),
+            vmem((2 * modes * SUBS, LANES), F32),
+            vmem((2 * modes * SUBS, LANES), F32),
+            vmem((chunks, 2 * modes, LANES), F32),
+            vmem((chunks, 2 * modes, LANES), F32),
             vmem((2 * modes, LANES), F32),
             vmem((LINE, 2 * modes, LANES), F32),
             vmem((2 * modes, LANES), F32),
@@ -672,7 +763,7 @@
             vmem((chunks, width, LANES), BF16),
             vmem((chunks, width, LANES), F32),
             vmem((chunks, width, LANES), F32),
-            dma((5,)),
+            dma((10,)),
             dma((chunks, 10)),
             dma((chunks, 10)),
             dma((1,)),
@@ -691,13 +782,13 @@
         return pl.pallas_call(
             functools.partial(mixer_kernel, (part_count, line_count)),
             out_shape=jax.ShapeDtypeStruct((width, rows), BF16),
-            in_specs=[hbm, near, hbm, near, near, near, near, hbm],
+            in_specs=[hbm] * 8,
             out_specs=near,
             scratch_shapes=scratch,
             compiler_params=pltpu.CompilerParams(collective_id=0, has_side_effects=True),
         )(
             tokens,
-            norm_gain[None, :],
+            norm_gain.reshape(depth // LANES, LANES),
             w_in,
             w_short,
             decay_rate,

time: 116 us -> 107 us (0.922)
  the two profiles are of different devices: /device:TPU:29 before, /device:TPU:25 now
where the time goes in v2:
time: 107 us
  Pallas kernels  106 us (99%)
  local copies, waits for them, and re-layouts  1.65 us (2%)
    pallas_call x1, Pallas kernels, body(): pl.pallas_call(functools.partial(mixer_kernel, (part_count, line_count)),...  106 us

profile of v2, /device:TPU:25, one launch (start us, length us, event | category | flops | bytes accessed | tf_op | source)
XLA Modules:
  0.0 107.3 jit_solution(16242934691705684122)
XLA Ops:
  0.0 105.6 %shard_map.82 = bf16[240,512]{1,0:T(8,128)(2,1)} custom-call(bf16[240,512]{1,0:T(8,128)(2,1)} %tokens.1, f32[15,128]{1,0:T(8,128)} %bitcast.2, bf16[3,240,1920]{2,1,0:T(8,128)(2,1)} %w_in.1, f32[3,3,240]{2,1,0:T(4,128)} %short_ref.1, f32[16,240]{1,0:T(8,128)} %decay_ref.1, f32[16,240]{1,0:T(8,128)} %residue_ref.1, f32[1,240]{1,0:T(1,128)} %bitcast.3, ...), custom_call_target="tpu_custom_call" | custom-call | tf_op jit(solution)/shard_map/pallas_call | solution.py:782
  105.6 1.7 %copy.10 = bf16[240,512]{1,0:T(8,128)(2,1)} copy(bf16[240,512]{1,0:T(8,128)(2,1)} %shard_map.82) | data formatting | bytes 491520
